TPU v7x, 512 devices: a whole 4x8x8 slice. The times are simulated.
512 devices in a mesh: leaf: 8 (over z), row: 8 (over y), col: 8 (over x, core).
Axes of the slice: x: 4, y: 8, z: 8, core: 2. Of those that a mesh axis runs over, the one named last changes fastest.
Arguments:
- child_inverse: bfloat16 [8, 2, 3072, 3072], P('leaf', None, 'row', 'col'), as said below
- child_rhs: bfloat16 [8, 2, 3072, 256], P('leaf', None, 'col'), may hold values from -6 to 6
- child_to_mid: bfloat16 [8, 2, 2048, 3072], P('leaf', None, ('row', 'col')), may hold values from -0.109375 to 0.109375
- child_to_root: bfloat16 [8, 2, 2048, 3072], P('leaf', None, ('row', 'col')), may hold values from -0.109375 to 0.109375
- mid_rows_list: int32 [8, 2, 2048], P('leaf'), may hold values from 0 to 4095, as said below
- root_rows_list: int32 [8, 2, 2048], P('leaf'), may hold values from 0 to 8191, as said below
- mid_inverse: bfloat16 [8, 4096, 4096], P('leaf', 'row', 'col'), as said below
- mid_rhs: bfloat16 [8, 4096, 256], P('leaf', 'col'), may hold values from -6 to 6
- mid_to_root: bfloat16 [8, 2048, 4096], P('leaf', ('row', 'col')), may hold values from -0.09375 to 0.09375
- mid_root_list: int32 [8, 2048], P('leaf'), may hold values from 0 to 8191, as said below
- root_inverse: bfloat16 [8192, 8192], P(('leaf', 'row'), 'col'), as said below
- root_rhs: bfloat16 [8192, 256], P('col'), may hold values from -6 to 6
Outputs:
- child_solution: bfloat16 [8, 2, 3072, 256], P('leaf', None, 'row')
- mid_solution: bfloat16 [8, 4096, 256], P('leaf', 'row')
- root_solution: bfloat16 [8192, 256], P(('leaf', 'row'))
Inputs may be any that keep to these rules, and one draw needn't show every extreme that they name: `mid_rows_list`: each list of a child holds 2048 distinct rows of its middle supernode in increasing order, always with the first and the last. `root_rows_list`: each list of a child holds 2048 distinct rows of the root in increasing order, always with the first and the last. `mid_root_list`: each list holds 2048 distinct rows of the root in increasing order, always with the first and the last. `child_inverse`: lower triangular with a positive diagonal. `mid_inverse`: lower triangular with a positive diagonal. `root_inverse`: lower triangular with a positive diagonal.
All inputs are finite; a program needn't handle non-finite values.
Results may differ from a plain program's by a relative error of at most 0.0085.
Values may be sent and summed in bfloat16 or wider, within the bound.
A program may use at most 64 MiB of HBM per device.

v0:
```python
import jax
import jax.numpy as jnp
from jax import lax
from jax.sharding import PartitionSpec as P


def solve_spread(partial_value):
    placed = lax.psum(partial_value, "col").astype(jnp.bfloat16)
    whole_rows = lax.all_gather(placed, "row", axis=2, tiled=True)
    return (placed, whole_rows)


def gather_updates(pieces):
    return lax.all_gather(pieces, ("row", "col"), axis=2, tiled=True)


def scatter_block(values, rows_list, piece_rows, col_index):
    width = values.shape[-1]
    flat_values = values.reshape(-1, width).astype(jnp.float32)
    offsets = rows_list.reshape(-1) - col_index * piece_rows
    inside = (offsets >= 0) & (offsets < piece_rows)
    target = jnp.where(inside, offsets, piece_rows)
    summed = jnp.zeros((piece_rows + 1, width), jnp.float32).at[target].add(flat_values)
    return summed[:piece_rows]


def per_device(
    child_inverse,
    child_rhs,
    child_to_mid,
    child_to_root,
    mid_rows_list,
    root_rows_list,
    mid_inverse,
    mid_rhs,
    mid_to_root,
    mid_root_list,
    root_inverse,
    root_rhs,
):
    grid_size = lax.axis_size("row") * lax.axis_size("col")
    col_index = lax.axis_index("col")
    rhs_width = child_rhs.shape[3]
    child_partial = jnp.einsum(
        "gcij,gcjr->gcir", child_inverse, child_rhs, preferred_element_type=jnp.float32
    )
    child_local, child_whole = solve_spread(child_partial)
    mid_piece = child_to_mid.shape[2]
    root_piece = child_to_root.shape[2]
    update_mid = jnp.einsum(
        "gcuj,gcjr->gcur", child_to_mid, child_whole, preferred_element_type=jnp.float32
    ).astype(jnp.bfloat16)
    update_root = jnp.einsum(
        "gcuj,gcjr->gcur", child_to_root, child_whole, preferred_element_type=jnp.float32
    ).astype(jnp.bfloat16)
    stacked = jnp.concatenate((update_mid, update_root), axis=2)
    gathered = gather_updates(stacked)
    lead_count = gathered.shape[0]
    child_count = gathered.shape[1]
    split_view = gathered.reshape(
        lead_count, child_count, grid_size, mid_piece + root_piece, rhs_width
    )
    mid_updates = split_view[:, :, :, :mid_piece].reshape(
        lead_count, child_count, grid_size * mid_piece, rhs_width
    )
    root_updates = split_view[:, :, :, mid_piece:].reshape(
        lead_count, child_count, grid_size * root_piece, rhs_width
    )
    root_group = root_rhs.shape[0]
    child_root_term = scatter_block(root_updates, root_rows_list, root_group, col_index)
    mid_term = scatter_block(mid_updates, mid_rows_list, mid_rhs.shape[1], col_index)
    mid_input = (mid_rhs[0].astype(jnp.float32) - mid_term).astype(jnp.bfloat16)
    mid_partial = jnp.dot(mid_inverse[0], mid_input, preferred_element_type=jnp.float32)[None, None]
    mid_local, mid_whole = solve_spread(mid_partial)
    update_top = jnp.dot(
        mid_to_root[0], mid_whole[0, 0], preferred_element_type=jnp.float32
    ).astype(jnp.bfloat16)[None, None]
    top_whole = gather_updates(update_top)
    top_term = scatter_block(top_whole, mid_root_list, root_group, col_index)
    root_sum = lax.psum(child_root_term + top_term, "leaf")
    root_input = (root_rhs.astype(jnp.float32) - root_sum).astype(jnp.bfloat16)
    root_partial = jnp.dot(root_inverse, root_input, preferred_element_type=jnp.float32)
    root_solution = lax.psum(root_partial, "col").astype(jnp.bfloat16)
    return (child_local, mid_local[0], root_solution)


def solution(mesh):
    in_specs = (
        P("leaf", None, "row", "col"),
        P("leaf", None, "col", None),
        P("leaf", None, ("row", "col"), None),
        P("leaf", None, ("row", "col"), None),
        P("leaf", None, None),
        P("leaf", None, None),
        P("leaf", "row", "col"),
        P("leaf", "col", None),
        P("leaf", ("row", "col"), None),
        P("leaf", None),
        P(("leaf", "row"), "col"),
        P("col", None),
    )
    out_specs = (P("leaf", None, "row", None), P("leaf", "row", None), P(("leaf", "row"), None))
    return jax.shard_map(
        per_device, mesh=mesh, in_specs=in_specs, out_specs=out_specs, check_vma=False
    )
```

profile of v0, /device:TPU:8, one launch (start us, length us, event | category | flops | bytes accessed | tf_op | source)
XLA Modules:
  0.0 500.9 jit_solution(5121878186767649496)
XLA Ops:
  7.2 0.0 all-gather.6.cloned.1.call-start
  7.2 1.0 copy-done
  8.2 1.4 convolution_bitcast_fusion
  9.6 32.4 %all-reduce.6 = bf16[1,2,384,256]{3,2,1,0:T(8,128)(2,1)} all-reduce(f32[1,2,384,256]{3,2,1,0:T(8,128)S(1)} %convolution_bitcast_fusion), channel_id=1, replica_groups=mesh['leaf'=8,'row'=8,'col'=8] {'col'}, use_global_device_ids=true, to_apply=%region_0.0 | all-reduce | flops 196608 | bytes 1179648 | tf_op jit(solution)/shard_map/psum | solution.py:8
  42.0 0.0 all-gather.6.cloned.1.call-update
  42.0 0.0 all-gather.8.cloned.1.call-start
  42.1 49.2 %all-gather.6.cloned.1.call-done = bf16[1,2,3072,256]{3,2,1,0:T(8,128)(2,1)} async-done(((bf16[1,2,384,256]{3,2,1,0:T(8,128)(2,1)}), bf16[1,2,3072,256]{3,2,1,0:T(8,128)(2,1)}) %all-gather.6.cloned.1.call-update) | async-done | bytes 3145744 | tf_op jit(solution)/shard_map/all_gather | solution.py:9
  91.3 2.7 fusion.18
  94.0 0.1 copy-done.1
  94.1 0.6 fusion.21
  94.8 0.6 pad_maximum_fusion
  95.5 0.0 all-gather.10.cloned.1.call-start
  95.6 82.8 %all-gather.8.cloned.1.call-done = bf16[1,2,4096,256]{3,2,1,0:T(8,128)(2,1)} async-done(((bf16[1,2,64,256]{3,2,1,0:T(8,128)(2,1)}), bf16[1,2,4096,256]{3,2,1,0:T(8,128)(2,1)}) %all-gather.8.cloned.1.call-update) | async-done | bytes 4194320 | tf_op jit(solution)/shard_map/all_gather | solution.py:14
  178.4 4.2 fusion.42
  182.6 28.5 %scatter_custom_fusion = f32[513,256]{1,0:T(8,128)S(1)} fusion(s32[4096]{0:T(1024)S(1)} %bitcast.88, bf16[4096,256]{1,0:T(8,128)(2,1)} %bitcast.83, f32[]{:T(128)} %constant.7.clone.1), kind=kCustom, calls=%fused_computation.5 | custom fusion | flops 2097152 | bytes 2622468 | tf_op jit(solution)/shard_map/scatter-add | solution.py:23
  211.2 2.2 convolution_bitcast_fusion.1
  213.4 32.1 %all-reduce.7 = bf16[1,1,512,256]{2,3,1,0:T(8,128)(2,1)} all-reduce(f32[1,1,512,256]{2,3,1,0:T(8,128)} %convolution_bitcast_fusion.1), channel_id=1, replica_groups=mesh['leaf'=8,'row'=8,'col'=8] {'col'}, use_global_device_ids=true, to_apply=%region_2.3 | all-reduce | flops 131072 | bytes 786432 | tf_op jit(solution)/shard_map/psum | solution.py:8
  245.4 0.0 all-gather.10.cloned.1.call-update
  245.5 0.0 all-gather.12.cloned.1.call-start
  245.5 40.1 %all-gather.10.cloned.1.call-done = bf16[1,1,4096,256]{2,3,1,0:T(8,128)(2,1)} async-done(((bf16[1,1,512,256]{2,3,1,0:T(8,128)(2,1)}), bf16[1,1,4096,256]{2,3,1,0:T(8,128)(2,1)}) %all-gather.10.cloned.1.call-update) | async-done | bytes 2097168 | tf_op jit(solution)/shard_map/all_gather | solution.py:9
  285.7 2.9 fusion.27
  288.6 0.0 all-gather.12.cloned.1.call-update
  288.6 0.0 all-reduce.5.cloned.1.call-start
  288.8 29.2 %scatter_custom_fusion.1 = f32[1025,256]{1,0:T(8,128)} fusion(s32[4096]{0:T(1024)S(1)} %bitcast.89, bf16[4096,256]{1,0:T(8,128)(2,1)S(1)} %bitcast.82, f32[]{:T(128)} %constant.7.clone.1), kind=kCustom, calls=%fused_computation.3 | custom fusion | flops 2097152 | bytes 3146756 | tf_op jit(solution)/shard_map/scatter-add | solution.py:23
  318.0 51.5 %all-gather.12.cloned.1.call-done = bf16[2048,256]{1,0:T(8,128)(2,1)} async-done(((bf16[32,256]{1,0:T(8,128)(2,1)}), bf16[2048,256]{1,0:T(8,128)(2,1)}) %all-gather.12.cloned.1.call-update) | async-done | bytes 1048592 | tf_op jit(solution)/shard_map/all_gather | solution.py:14
  369.5 14.9 %scatter_custom_fusion.2 = f32[1025,256]{1,0:T(8,128)S(1)} fusion(s32[2048]{0:T(1024)S(1)} %bitcast.90, bf16[2048,256]{1,0:T(8,128)(2,1)} %all-gather.12.cloned.1.call-done, f32[]{:T(128)} %constant.7.clone.1), kind=kCustom, calls=%fused_computation.13 | custom fusion | flops 1048576 | bytes 2098180 | tf_op jit(solution)/shard_map/scatter-add | solution.py:23
  384.4 1.2 slice_add_fusion
  385.6 0.8 copy.17
  386.5 80.8 %all-reduce.5.cloned.1.call-done = f32[1024,256]{1,0:T(8,128)} async-done(((f32[1024,256]{1,0:T(8,128)}), f32[1024,256]{1,0:T(8,128)}) %all-reduce.5.cloned.1.call-update) | async-done | bytes 1048592 | tf_op jit(solution)/shard_map/psum | solution.py:80
  467.3 1.6 convolution_bitcast_fusion.2
  468.9 24.7 %all-reduce.8 = bf16[128,256]{0,1:T(8,128)(2,1)S(1)} all-reduce(f32[128,256]{0,1:T(8,128)S(1)} %convolution_bitcast_fusion.2), channel_id=1, replica_groups=mesh['leaf'=8,'row'=8,'col'=8] {'col'}, use_global_device_ids=true, to_apply=%region_6.7 | all-reduce | flops 32768 | bytes 196608 | tf_op jit(solution)/shard_map/psum | solution.py:83
  493.6 0.7 copy.18
  (29 shorter events, 0.2 us)
Async XLA Ops:
  7.2 1.1 copy-start
  7.2 84.1 %copy-start.5 = (bf16[1,2,32,3072]{3,2,1,0:T(8,128)(2,1)S(1)}, bf16[1,2,32,3072]{3,2,1,0:T(8,128)(2,1)}, u32[]{:S(2)}) copy-start(bf16[1,2,32,3072]{3,2,1,0:T(8,128)(2,1)} %param.14) | copy-start | bytes 1179652
  7.2 84.1 %all-gather.6.cloned.1.call-start = ((), (), s32[]{:S(2)}) async-start(), calls=%async_computation | async-start | bytes 3538944 | tf_op jit(solution)/shard_map/all_gather | solution.py:9
  42.0 52.0 %copy-start.6 = (bf16[1,2,32,3072]{3,2,1,0:T(8,128)(2,1)S(1)}, bf16[1,2,32,3072]{3,2,1,0:T(8,128)(2,1)}, u32[]{:S(2)}) copy-start(bf16[1,2,32,3072]{3,2,1,0:T(8,128)(2,1)} %param.15) | copy-start | bytes 1179652
  42.0 136.4 %all-gather.8.cloned.1.call-start = ((), (), s32[]{:S(2)}) async-start(), calls=%async_computation.1 | async-start | bytes 4259840 | tf_op jit(solution)/shard_map/all_gather | solution.py:14
  91.3 2.8 copy-start.1
  94.1 1.4 copy-start.8
  95.5 190.2 %all-gather.10.cloned.1.call-start = ((), (), s32[]{:S(2)}) async-start(), calls=%async_computation.2 | async-start | bytes 2359296 | tf_op jit(solution)/shard_map/all_gather | solution.py:9
  182.6 28.5 %copy-start.7 = (bf16[1,512,256]{2,1,0:T(8,128)(2,1)S(1)}, bf16[1,512,256]{2,1,0:T(8,128)(2,1)}, u32[]{:S(2)}) copy-start(bf16[1,512,256]{2,1,0:T(8,128)(2,1)} %param.19) | copy-start | bytes 786436
  213.4 75.3 %copy-start.9 = (s32[1,2,2048]{2,1,0:T(2,128)S(1)}, s32[1,2,2048]{2,1,0:T(2,128)}, u32[]{:S(2)}) copy-start(s32[1,2,2048]{2,1,0:T(2,128)} %param.17) | copy-start | bytes 49156
  213.4 75.4 %copy-start.10 = (s32[1,2048]{1,0:T(1,128)S(1)}, s32[1,2048]{1,0:T(1,128)}, u32[]{:S(2)}) copy-start(s32[1,2048]{1,0:T(1,128)} %param.21) | copy-start | bytes 24580
  245.5 124.1 %all-gather.12.cloned.1.call-start = ((), (), s32[]{:S(2)}) async-start(), calls=%async_computation.4 | async-start | bytes 1064960 | tf_op jit(solution)/shard_map/all_gather | solution.py:14
  288.6 178.7 %all-reduce.5.cloned.1.call-start = ((), (), s32[]{:S(2)}) async-start(), calls=%async_computation.3 | async-start | bytes 2097152 | tf_op jit(solution)/shard_map/psum | solution.py:80
  318.0 66.4 %copy-start.2 = (f32[1025,256]{1,0:T(8,128)S(1)}, f32[1025,256]{1,0:T(8,128)}, u32[]{:S(2)}) copy-start(f32[1025,256]{1,0:T(8,128)} %scatter_custom_fusion.1) | copy-start | bytes 3148804
  384.4 1.2 copy-start.3
  384.4 82.9 %copy-start.4 = (bf16[1024,256]{1,0:T(8,128)(2,1)S(1)}, bf16[1024,256]{1,0:T(8,128)(2,1)}, u32[]{:S(2)}) copy-start(bf16[1024,256]{1,0:T(8,128)(2,1)} %param.23) | copy-start | bytes 1572868
Sparse Core Ops, SparseCore 0:
  42.2 49.0 all-gather.5
  95.6 82.8 all-gather.7
  245.6 40.0 all-gather.9
  289.4 80.0 all-gather.11
  385.8 81.4 all-reduce.4
where the time goes:
time: 501 us
  waiting for transfers between devices  305 us (61%)
  blocking collectives  89.2 us (18%)
  other arithmetic  74.5 us (15%)
  between operations  14 us (3%)
  matrix products  11.4 us (2%)
  local copies, waits for them, and re-layouts  7.04 us (1%)
    all_gather x2, waiting for transfers between devices, gather_updates(): return lax.all_gather(pieces, ('row', 'col'), axis=2, tiled=True)  134 us
    all_gather x2, waiting for transfers between devices, solve_spread(): whole_rows = lax.all_gather(placed, 'row', axis=2, tiled=True)  89.3 us
    psum x1, waiting for transfers between devices, per_device(): root_sum = lax.psum(child_root_term + top_term, 'leaf')  80.8 us
    scatter-add x3, other arithmetic, scatter_block(): jnp.zeros((piece_rows + 1, width), jnp.float32).at[target].add(flat_values)  72.6 us
    psum x2, blocking collectives, solve_spread(): placed = lax.psum(partial_value, 'col').astype(jnp.bfloat16)  64.5 us
    psum x1, blocking collectives, per_device(): root_solution = lax.psum(root_partial, 'col').astype(jnp.bfloat16)  24.7 us
  transfers between devices with their start and end apart: 5, of which 5 were waited for; matrix products, arithmetic and copies ran while one was open for 6% of the time, Pallas kernels for 0%

commit v1 on v0

--- a/solution.py
+++ b/solution.py
@@ -77,7 +77,7 @@
     ).astype(jnp.bfloat16)[None, None]
     top_whole = gather_updates(update_top)
     top_term = scatter_block(top_whole, mid_root_list, root_group, col_index)
-    root_sum = lax.psum(child_root_term + top_term, "leaf")
+    root_sum = jnp.sum(lax.all_gather(child_root_term + top_term, "leaf"), axis=0)
     root_input = (root_rhs.astype(jnp.float32) - root_sum).astype(jnp.bfloat16)
     root_partial = jnp.dot(root_inverse, root_input, preferred_element_type=jnp.float32)
     root_solution = lax.psum(root_partial, "col").astype(jnp.bfloat16)

time: 501 us -> 521 us (1.040)
  waiting for transfers between devices: 305 us -> 320 us
    all_gather x0 -> x1, waiting for transfers between devices: none -> 95.9 us  [per_device(): lax.all_gather(child_root_term + top_term, 'leaf')]
    psum x1 -> x0, waiting for transfers between devices: 80.8 us -> none  [per_device(): root_sum = lax.psum(child_root_term + top_term, 'leaf')]
where the time goes in v1:
time: 521 us
  waiting for transfers between devices  320 us (61%)
  blocking collectives  91.1 us (17%)
  other arithmetic  78.6 us (15%)
  between operations  14 us (3%)
  matrix products  10.2 us (2%)
  local copies, waits for them, and re-layouts  7.05 us (1%)
    all_gather x2, waiting for transfers between devices, gather_updates(): return lax.all_gather(pieces, ('row', 'col'), axis=2, tiled=True)  134 us
    all_gather x1, waiting for transfers between devices, per_device(): lax.all_gather(child_root_term + top_term, 'leaf')  95.9 us
    all_gather x2, waiting for transfers between devices, solve_spread(): whole_rows = lax.all_gather(placed, 'row', axis=2, tiled=True)  89.4 us
    scatter-add x3, other arithmetic, scatter_block(): jnp.zeros((piece_rows + 1, width), jnp.float32).at[target].add(flat_values)  72.6 us
    psum x2, blocking collectives, solve_spread(): placed = lax.psum(partial_value, 'col').astype(jnp.bfloat16)  64.5 us
    psum x1, blocking collectives, per_device(): root_solution = lax.psum(root_partial, 'col').astype(jnp.bfloat16)  26.6 us
  transfers between devices with their start and end apart: 5, of which 5 were waited for; matrix products, arithmetic and copies ran while one was open for 6% of the time, Pallas kernels for 0%

profile of v1, /device:TPU:8, one launch (start us, length us, event | category | flops | bytes accessed | tf_op | source)
XLA Modules:
  0.0 520.8 jit_solution(7180553577764983337)
XLA Ops:
  7.2 0.0 all-gather.8.cloned.1.call-start
  7.2 1.0 copy-done
  8.2 1.4 convolution_bitcast_fusion
  9.6 32.4 %all-reduce.3 = bf16[1,2,384,256]{3,2,1,0:T(8,128)(2,1)} all-reduce(f32[1,2,384,256]{3,2,1,0:T(8,128)S(1)} %convolution_bitcast_fusion), channel_id=1, replica_groups=mesh['leaf'=8,'row'=8,'col'=8] {'col'}, use_global_device_ids=true, to_apply=%region_0.0 | all-reduce | flops 196608 | bytes 1179648 | tf_op jit(solution)/shard_map/psum | solution.py:8
  42.0 0.0 all-gather.8.cloned.1.call-update
  42.0 0.0 all-gather.10.cloned.1.call-start
  42.1 49.2 %all-gather.8.cloned.1.call-done = bf16[1,2,3072,256]{3,2,1,0:T(8,128)(2,1)} async-done(((bf16[1,2,384,256]{3,2,1,0:T(8,128)(2,1)}), bf16[1,2,3072,256]{3,2,1,0:T(8,128)(2,1)}) %all-gather.8.cloned.1.call-update) | async-done | bytes 3145744 | tf_op jit(solution)/shard_map/all_gather | solution.py:9
  91.3 2.7 fusion.21
  94.0 0.1 copy-done.1
  94.1 0.6 fusion.18
  94.8 0.6 pad_maximum_fusion
  95.4 0.0 all-gather.10.cloned.1.call-update
  95.5 0.0 all-gather.12.cloned.1.call-start
  95.6 82.8 %all-gather.10.cloned.1.call-done = bf16[1,2,4096,256]{3,2,1,0:T(8,128)(2,1)} async-done(((bf16[1,2,64,256]{3,2,1,0:T(8,128)(2,1)}), bf16[1,2,4096,256]{3,2,1,0:T(8,128)(2,1)}) %all-gather.10.cloned.1.call-update) | async-done | bytes 4194320 | tf_op jit(solution)/shard_map/all_gather | solution.py:14
  178.4 4.2 fusion.42
  182.7 28.5 %scatter_custom_fusion = f32[513,256]{1,0:T(8,128)S(1)} fusion(s32[4096]{0:T(1024)S(1)} %bitcast.90, bf16[4096,256]{1,0:T(8,128)(2,1)} %bitcast.85, f32[]{:T(128)} %constant.7.clone.1), kind=kCustom, calls=%fused_computation.5 | custom fusion | flops 2097152 | bytes 2622468 | tf_op jit(solution)/shard_map/scatter-add | solution.py:23
  211.2 2.2 convolution_bitcast_fusion.1
  213.4 32.1 %all-reduce.4 = bf16[1,1,512,256]{2,3,1,0:T(8,128)(2,1)} all-reduce(f32[1,1,512,256]{2,3,1,0:T(8,128)} %convolution_bitcast_fusion.1), channel_id=1, replica_groups=mesh['leaf'=8,'row'=8,'col'=8] {'col'}, use_global_device_ids=true, to_apply=%region_2.3 | all-reduce | flops 131072 | bytes 786432 | tf_op jit(solution)/shard_map/psum | solution.py:8
  245.5 0.0 all-gather.14.cloned.1.call-start
  245.5 40.1 %all-gather.12.cloned.1.call-done = bf16[1,1,4096,256]{2,3,1,0:T(8,128)(2,1)} async-done(((bf16[1,1,512,256]{2,3,1,0:T(8,128)(2,1)}), bf16[1,1,4096,256]{2,3,1,0:T(8,128)(2,1)}) %all-gather.12.cloned.1.call-update) | async-done | bytes 2097168 | tf_op jit(solution)/shard_map/all_gather | solution.py:9
  285.7 2.9 fusion.27
  288.6 0.0 all-gather.16.cloned.1.call-start
  288.8 29.2 %scatter_custom_fusion.1 = f32[1025,256]{1,0:T(8,128)} fusion(s32[4096]{0:T(1024)S(1)} %bitcast.91, bf16[4096,256]{1,0:T(8,128)(2,1)S(1)} %bitcast.84, f32[]{:T(128)} %constant.7.clone.1), kind=kCustom, calls=%fused_computation.3 | custom fusion | flops 2097152 | bytes 3146756 | tf_op jit(solution)/shard_map/scatter-add | solution.py:23
  318.0 51.5 %all-gather.14.cloned.1.call-done = bf16[2048,256]{1,0:T(8,128)(2,1)} async-done(((bf16[32,256]{1,0:T(8,128)(2,1)}), bf16[2048,256]{1,0:T(8,128)(2,1)}) %all-gather.14.cloned.1.call-update) | async-done | bytes 1048592 | tf_op jit(solution)/shard_map/all_gather | solution.py:14
  369.6 14.9 %scatter_custom_fusion.2 = f32[1025,256]{1,0:T(8,128)S(1)} fusion(s32[2048]{0:T(1024)S(1)} %bitcast.92, bf16[2048,256]{1,0:T(8,128)(2,1)} %all-gather.14.cloned.1.call-done, f32[]{:T(128)} %constant.7.clone.1), kind=kCustom, calls=%fused_computation.13 | custom fusion | flops 1048576 | bytes 2098180 | tf_op jit(solution)/shard_map/scatter-add | solution.py:23
  384.4 1.2 slice_add_fusion
  385.7 0.8 copy.17
  386.5 95.9 %all-gather.16.cloned.1.call-done = f32[8192,256]{1,0:T(8,128)} async-done(((f32[1024,256]{1,0:T(8,128)}), f32[8192,256]{1,0:T(8,128)}) %all-gather.16.cloned.1.call-update) | async-done | bytes 8388624 | tf_op jit(solution)/shard_map/all_gather | solution.py:80
  482.4 4.1 reduce_sum.9
  486.5 0.4 convolution_bitcast_fusion.2
  486.9 26.6 %all-reduce.5 = bf16[128,256]{0,1:T(8,128)(2,1)S(1)} all-reduce(f32[128,256]{0,1:T(8,128)S(1)} %convolution_bitcast_fusion.2), channel_id=1, replica_groups=mesh['leaf'=8,'row'=8,'col'=8] {'col'}, use_global_device_ids=true, to_apply=%region_6.7 | all-reduce | flops 32768 | bytes 196608 | tf_op jit(solution)/shard_map/psum | solution.py:83
  513.5 0.7 copy.18
  (32 shorter events, 0.2 us)
Async XLA Ops:
  7.2 1.1 copy-start
  7.2 84.1 %copy-start.5 = (bf16[1,2,32,3072]{3,2,1,0:T(8,128)(2,1)S(1)}, bf16[1,2,32,3072]{3,2,1,0:T(8,128)(2,1)}, u32[]{:S(2)}) copy-start(bf16[1,2,32,3072]{3,2,1,0:T(8,128)(2,1)} %param.15) | copy-start | bytes 1179652
  7.2 84.1 %all-gather.8.cloned.1.call-start = ((), (), s32[]{:S(2)}) async-start(), calls=%async_computation | async-start | bytes 3538944 | tf_op jit(solution)/shard_map/all_gather | solution.py:9
  42.0 52.0 %copy-start.6 = (bf16[1,2,32,3072]{3,2,1,0:T(8,128)(2,1)S(1)}, bf16[1,2,32,3072]{3,2,1,0:T(8,128)(2,1)}, u32[]{:S(2)}) copy-start(bf16[1,2,32,3072]{3,2,1,0:T(8,128)(2,1)} %param.14) | copy-start | bytes 1179652
  42.0 136.4 %all-gather.10.cloned.1.call-start = ((), (), s32[]{:S(2)}) async-start(), calls=%async_computation.1 | async-start | bytes 4259840 | tf_op jit(solution)/shard_map/all_gather | solution.py:14
  91.3 2.8 copy-start.1
  94.1 1.4 copy-start.9
  95.5 190.2 %all-gather.12.cloned.1.call-start = ((), (), s32[]{:S(2)}) async-start(), calls=%async_computation.2 | async-start | bytes 2359296 | tf_op jit(solution)/shard_map/all_gather | solution.py:9
  182.7 28.5 %copy-start.7 = (bf16[1,512,256]{2,1,0:T(8,128)(2,1)S(1)}, bf16[1,512,256]{2,1,0:T(8,128)(2,1)}, u32[]{:S(2)}) copy-start(bf16[1,512,256]{2,1,0:T(8,128)(2,1)} %param.19) | copy-start | bytes 786436
  213.4 75.3 %copy-start.10 = (s32[1,2,2048]{2,1,0:T(2,128)S(1)}, s32[1,2,2048]{2,1,0:T(2,128)}, u32[]{:S(2)}) copy-start(s32[1,2,2048]{2,1,0:T(2,128)} %param.17) | copy-start | bytes 49156
  213.4 75.4 %copy-start.11 = (s32[1,2048]{1,0:T(1,128)S(1)}, s32[1,2048]{1,0:T(1,128)}, u32[]{:S(2)}) copy-start(s32[1,2048]{1,0:T(1,128)} %param.21) | copy-start | bytes 24580
  245.5 124.1 %all-gather.14.cloned.1.call-start = ((), (), s32[]{:S(2)}) async-start(), calls=%async_computation.3 | async-start | bytes 1064960 | tf_op jit(solution)/shard_map/all_gather | solution.py:14
  288.6 193.7 %all-gather.16.cloned.1.call-start = ((), (), s32[]{:S(2)}) async-start(), calls=%async_computation.4 | async-start | bytes 9437184 | tf_op jit(solution)/shard_map/all_gather | solution.py:80
  318.0 66.4 %copy-start.2 = (f32[1025,256]{1,0:T(8,128)S(1)}, f32[1025,256]{1,0:T(8,128)}, u32[]{:S(2)}) copy-start(f32[1025,256]{1,0:T(8,128)} %scatter_custom_fusion.1) | copy-start | bytes 3148804
  384.4 1.2 copy-start.3
  482.4 4.1 copy-start.4
  482.4 4.1 copy-start.8
Sparse Core Ops, SparseCore 0:
  42.2 49.0 all-gather.7
  95.6 82.8 all-gather.9
  245.6 40.0 all-gather.11
  289.4 80.0 all-gather.13
  385.8 96.5 all-gather.15
